TPU v7x, 32 devices: a whole 2x2x4 slice. The times are simulated.
32 devices in a mesh: row: 4 (over y, core), col: 8 (over z, x).
Axes of the slice: x: 2, y: 2, z: 4, core: 2. Of those that a mesh axis runs over, the one named last changes fastest.
Arguments:
- factor: float32 [24, 262144], P(None, ('row', 'col')), may hold values from -1.2 to 1.2
- prior: float32 [24, 262144], P(None, ('row', 'col')), may hold values from -1.2 to 1.2
- tile_src: int32 [32, 384], P(('row', 'col')), may hold values from 0 to 63
- tile_dst: int32 [32, 384], P(('row', 'col')), may hold values from 0 to 63
- tile_count: int32 [32], P(('row', 'col')), may hold values from 96 to 384, as said below
- tile_vals: bfloat16 [12288, 128, 128], P(('row', 'col'))
- sep_idx: int32 [32, 4, 256], P(('row', 'col')), may hold values from 0 to 8191, as said below
- sep_count: int32 [32, 4], P(('row', 'col')), may hold values from 64 to 256, as said below
- couple: bfloat16 [32, 4, 256, 256], P(('row', 'col')), may hold values from -0.1875 to 0.1875
- masks: int32 [4], replicated, may hold values from 1 to 31, as said below
Outputs:
- new_factor: float32 [24, 262144], P(None, ('row', 'col'))
- momentum: float32 [], replicated
- energy: float32 [], replicated
Inputs may be any that keep to these rules, and one draw needn't show every extreme that they name: `tile_count`: some partition has all 384 slots live; slots at or beyond a partition's count are padding. `sep_idx`: distinct within one partition and round. `sep_count`: in every round some partition has all 256 slots live. masks[0] is 31, masks[1] is 16 and the last round's mask is 1.
All inputs are finite; a program needn't handle non-finite values.
Results may differ from a plain program's by a relative error of at most 0.0031.
Values may be sent and summed in bfloat16 or wider, within the bound.
A program may use at most 128 MiB of HBM per device.

v0:
```python
import functools

import jax
import jax.numpy as jnp
from jax import lax
from jax.experimental import pallas as pl
from jax.experimental.pallas import tpu as pltpu
from jax.sharding import PartitionSpec as P

TILE = 128
ITERS = 2
MOMENTUM_CAP = 0.9
MESH = pl.DeviceIdType.MESH
LIMIT = 60 * 1024 * 1024
UNROLL = 8
BANKS = 1
SHIFT = 16
GROUP = 16


def flip(x, j):
    bit = 1
    while bit <= j:
        if j & bit:
            x = x + bit * (1 - 2 * ((x // bit) % 2))
        bit *= 2
    return x


def step_kernel(mode, rows, cols, nodes_all, *refs):
    first, last = mode == "first", mode == "last"
    parts = rows * cols
    refs = list(refs)
    take = lambda n: [refs.pop(0) for _ in range(n)]
    if not last:
        idx_ref, cnt_ref, masks_ref = take(3)
    if first:
        cur_ref, prior_ref = take(2)
    elif last:
        part_ref = take(1)[0]
    else:
        cur_ref, blend_ref, app_ref = take(3)
        new_ref = take(1)[0]
    if not last:
        nblend_ref, recv_ref = take(2)
    else:
        beta_ref, energy_ref = take(2)
    if not first:
        stat, srow, scol = take(3)
        st_send, st_rrow, st_rcol = take(3)
    if not last:
        xt, gt, sbuf, direct, brow, bcol, picked = take(7)
        d_send, d_recv, c_send, c_recv, r_send, r_recv = take(6)

    if not last:
        comps = cur_ref.shape[0]
        blocks = cur_ref.shape[1] // TILE
    r = lax.axis_index("row")
    c = lax.axis_index("col")

    barrier = pltpu.get_barrier_semaphore()
    peers = [(flip(r, j), c) for j in range(1, rows)] + [(r, flip(c, j)) for j in range(1, cols)]
    if not last:
        peers.append((flip(r, rows - 1), flip(c, cols - 1)))
    for peer in peers:
        pl.semaphore_signal(barrier, inc=1, device_id=peer, device_id_type=MESH)

    def lanes(b):
        return pl.ds(pl.multiple_of(b * TILE, TILE), TILE)

    if not last:
        _, rounds, slots = idx_ref.shape
        slot_range = lax.broadcasted_iota(jnp.int32, (1, slots), 1)

        def gather_round(k):
            for j in range(slots):
                gt[j:j + 1, :] = xt[pl.ds(idx_ref[0, k, j], 1), :]
            sbuf[k] = jnp.where(slot_range < cnt_ref[0, k], gt[...].T, 0.0).astype(jnp.bfloat16)

    def first_block(b, carry):
        blend = cur_ref[:, lanes(b)] + beta0 * (cur_ref[:, lanes(b)] - prior_ref[:, lanes(b)])
        nblend_ref[:, lanes(b)] = blend
        xt[lanes(b), :] = blend.T
        return carry

    def norm_block(b, carry):
        change, total = carry
        applied = app_ref[:, lanes(b)]
        moved = blend_ref[:, lanes(b)] + applied
        length = jnp.sqrt(jnp.sum(moved * moved, axis=0, keepdims=True))
        updated = moved / jnp.maximum(length, 1.0)
        delta = updated - cur_ref[:, lanes(b)]
        new_ref[:, lanes(b)] = updated
        xt[lanes(b), :] = jnp.concatenate([updated, delta], axis=0).T
        return (change + applied * delta, total + applied * updated)

    def stat_copy(stage, slot, q):
        src, dst = stat.at[stage], (srow, scol)[stage].at[slot]
        recv = (st_rrow, st_rcol)[stage].at[slot]
        where = (q, c) if stage == 0 else (r, q)
        return src, dst, recv, where

    def stat_send(stage):
        size, mine = ((rows, r), (cols, c))[stage]
        sent = []
        for j in range(1, size):
            src, dst, recv, where = stat_copy(stage, mine, flip(mine, j))
            sent.append(pltpu.make_async_remote_copy(
                src_ref=src, dst_ref=dst, send_sem=st_send.at[stage * rows + j], recv_sem=recv,
                device_id=where, device_id_type=MESH))
            sent[-1].start()
        return sent

    def stat_take(stage):
        size, mine = ((rows, r), (cols, c))[stage]
        for j in range(1, size):
            q = flip(mine, j)
            src, dst, recv, where = stat_copy(stage, q, q)
            pltpu.make_async_remote_copy(
                src_ref=src, dst_ref=dst, send_sem=st_send.at[stage * rows + j], recv_sem=recv,
                device_id=where, device_id_type=MESH).wait_recv()
        own = stat[stage]
        slots_in = (srow, scol)[stage]
        every = jnp.where(mine == 0, own, slots_in[0])
        for q in range(1, size):
            every = every + jnp.where(mine == q, own, slots_in[q])
        return every

    def stat_beta(every):
        sums = jnp.sum(every, axis=1, keepdims=True) / nodes_all
        return MOMENTUM_CAP * 0.5 * (1.0 + jnp.tanh(sums[0:1])), sums[1:2]

    beta0 = 0.5 * MOMENTUM_CAP
    stat_sends = []
    if first:
        lax.fori_loop(0, blocks, first_block, 0, unroll=4)
        pl.semaphore_wait(barrier, len(peers))
    else:
        stat[...] = jnp.zeros_like(stat)
        if last:
            stat[0] = part_ref[...]
        else:
            zero = jnp.zeros((comps, TILE), jnp.float32)
            change, total = lax.fori_loop(0, blocks, norm_block, (zero, zero), unroll=4)
            stat[0, 0:1, :] = jnp.sum(change, axis=0, keepdims=True)
            stat[0, 1:2, :] = jnp.sum(total, axis=0, keepdims=True)
        pl.semaphore_wait(barrier, len(peers))
        stat_sends += stat_send(0)
        if last:
            stat[1] = stat_take(0)
            stat_sends += stat_send(1)
            beta, energy = stat_beta(stat_take(1))
            beta_ref[...] = jnp.broadcast_to(beta, beta_ref.shape)
            energy_ref[...] = jnp.broadcast_to(energy, energy_ref.shape)
            for copy in stat_sends:
                copy.wait_send()
            return

    def fixed(k):
        if k == 0:
            return parts - 1
        if k == 1:
            return parts // 2
        return 1 if k == rounds - 1 else None

    loose = [k for k in range(rounds) if fixed(k) is None]
    firm = [k for k in range(rounds) if fixed(k) is not None]

    def direct_copy(k):
        mask = fixed(k)
        return pltpu.make_async_remote_copy(
            src_ref=sbuf.at[k], dst_ref=direct.at[k], send_sem=d_send.at[k], recv_sem=d_recv.at[k],
            device_id=(flip(r, mask // cols), flip(c, mask % cols)), device_id_type=MESH)

    sends = []
    for n, k in enumerate(loose):
        gather_round(k)
        for j in range(1, cols):
            sends.append(pltpu.make_async_remote_copy(
                src_ref=sbuf.at[k], dst_ref=bcol.at[n, j], send_sem=c_send.at[n, j], recv_sem=c_recv.at[n, j],
                device_id=(r, flip(c, j)), device_id_type=MESH))
            sends[-1].start()
        bcol[n, 0] = sbuf[k]
    if not first:
        stat[1] = stat_take(0)
        stat_sends += stat_send(1)
    for k in firm:
        gather_round(k)
        copy = direct_copy(k)
        copy.start()
    if not first:
        beta, _ = stat_beta(stat_take(1))

        def blend_block(b, carry):
            now = new_ref[:, lanes(b)]
            nblend_ref[:, lanes(b)] = now + beta * (now - cur_ref[:, lanes(b)])
            return carry

        lax.fori_loop(0, blocks, blend_block, 0, unroll=4)

    def taken(block):
        if first:
            return block
        whole = block.astype(jnp.float32)
        return (whole[:comps] + beta * whole[comps:]).astype(jnp.bfloat16)

    col_sends = list(sends)
    row_sends = []
    for n, k in enumerate(loose):
        for copy in col_sends[n * (cols - 1):(n + 1) * (cols - 1)]:
            copy.wait_recv()
        picked[n] = bcol[n, masks_ref[k] % cols]
        for j in range(1, rows):
            copy = pltpu.make_async_remote_copy(
                src_ref=picked.at[n], dst_ref=brow.at[n, j], send_sem=r_send.at[n, j], recv_sem=r_recv.at[n, j],
                device_id=(flip(r, j), c), device_id_type=MESH)
            copy.start()
            row_sends.append(copy)
        brow[n, 0] = picked[n]
    for n, k in enumerate(loose):
        for copy in row_sends[n * (rows - 1):(n + 1) * (rows - 1)]:
            copy.wait_recv()
        recv_ref[k] = taken(brow[n, masks_ref[k] // cols])
    for k in firm:
        direct_copy(k).wait_recv()
        recv_ref[k] = taken(direct[k])
    for copy in stat_sends + col_sends + row_sends:
        copy.wait_send()
    for k in firm:
        direct_copy(k).wait_send()


def step(mode, rows, cols, nodes_all, cid, smalls, arrays):
    vm = pl.BlockSpec(memory_space=pltpu.VMEM)
    sm = pl.BlockSpec(memory_space=pltpu.SMEM)
    comps, nodes = arrays[0].shape
    f32, bf16 = jnp.float32, jnp.bfloat16
    dma = pltpu.SemaphoreType.DMA
    outs, scratch = [], []
    if mode != "first":
        if mode != "last":
            outs.append(jax.ShapeDtypeStruct((comps, nodes), f32))
        scratch += [pltpu.VMEM((2, 8, TILE), f32), pltpu.VMEM((rows, 8, TILE), f32), pltpu.VMEM((cols, 8, TILE), f32)]
        scratch += [dma((rows + cols,)), dma((rows,)), dma((cols,))]
    if mode != "last":
        _, rounds, slots = smalls[0].shape
        loose = max(rounds - 3, 1)
        outs.append(jax.ShapeDtypeStruct((comps, nodes), f32))
        outs.append(jax.ShapeDtypeStruct((rounds, comps, slots), bf16))
        wide = comps if mode == "first" else 2 * comps
        scratch += [pltpu.VMEM((nodes, wide), f32), pltpu.VMEM((slots, wide), f32)]
        scratch += [pltpu.VMEM((rounds, wide, slots), bf16), pltpu.VMEM((rounds, wide, slots), bf16)]
        scratch += [pltpu.VMEM((loose, rows, wide, slots), bf16), pltpu.VMEM((loose, cols, wide, slots), bf16)]
        scratch += [pltpu.VMEM((loose, wide, slots), bf16)]
        scratch += [dma((rounds,)), dma((rounds,)), dma((loose, cols)), dma((loose, cols)), dma((loose, rows)), dma((loose, rows))]
    else:
        outs += [jax.ShapeDtypeStruct((1, TILE), f32)] * 2
    return pl.pallas_call(
        functools.partial(step_kernel, mode, rows, cols, nodes_all),
        out_shape=outs,
        in_specs=[sm] * len(smalls) + [vm] * len(arrays),
        out_specs=[vm] * len(outs),
        scratch_shapes=scratch,
        compiler_params=pltpu.CompilerParams(collective_id=cid, has_side_effects=True, vmem_limit_bytes=LIMIT),
        name="step_" + mode,
    )(*smalls, *arrays)


def apply_kernel(chunk, last, code_ref, idx_ref, cnt_ref, vals_ref, blend_ref, recv_ref, couple_ref, *refs):
    if last:
        cur_ref, out_ref, stat_ref, *acc, at, ext = refs
    else:
        out_ref, *acc, at, ext = refs
    pid = pl.program_id(0)
    comps, nodes = blend_ref.shape
    blocks = nodes // TILE
    _, rounds, slots = idx_ref.shape

    @pl.when(pid == 0)
    def _():
        for bank in acc:
            bank[...] = jnp.zeros_like(bank)

    for base in range(0, chunk, UNROLL):
        prods = []
        for t in range(base, base + UNROLL, 2):
            spots = [pl.ds(pl.multiple_of((code_ref[pid, t + i] & ((1 << SHIFT) - 1)) * TILE, TILE), TILE) for i in range(2)]
            pair = jnp.concatenate([blend_ref[:, spot] for spot in spots], axis=0).astype(jnp.bfloat16)
            side = jnp.concatenate([vals_ref[t], vals_ref[t + 1]], axis=1)
            both = jnp.dot(pair, side, preferred_element_type=jnp.float32)
            prods += [both[:comps, :TILE], both[comps:, TILE:]]
        for t in range(base, base + UNROLL):
            acc[t % BANKS][code_ref[pid, t] >> SHIFT] += prods[t - base]

    @pl.when(pid == pl.num_programs(0) - 1)
    def _():
        at[...] = jnp.zeros_like(at)
        slot_range = lax.broadcasted_iota(jnp.int32, (1, slots), 1)
        for k in range(rounds):
            extra = jnp.dot(recv_ref[k], couple_ref[k], preferred_element_type=jnp.float32)
            ext[...] = jnp.where(slot_range < cnt_ref[0, k], extra, 0.0).T
            for base in range(0, slots, GROUP):
                where = [idx_ref[0, k, base + i] for i in range(GROUP)]
                sums = [at[pl.ds(where[i], 1), :] + ext[base + i:base + i + 1, :] for i in range(GROUP)]
                for i in range(GROUP):
                    at[pl.ds(where[i], 1), :] = sums[i]

        def applied_at(b):
            span = pl.ds(pl.multiple_of(b * TILE, TILE), TILE)
            return span, sum(bank[b] for bank in acc) + at[span, :].T

        if not last:
            def finish(b, carry):
                span, applied = applied_at(b)
                out_ref[:, span] = applied
                return carry

            lax.fori_loop(0, blocks, finish, 0, unroll=4)
        else:
            def finish(b, carry):
                change, total = carry
                span, applied = applied_at(b)
                moved = blend_ref[:, span] + applied
                length = jnp.sqrt(jnp.sum(moved * moved, axis=0, keepdims=True))
                updated = moved / jnp.maximum(length, 1.0)
                out_ref[:, span] = updated
                return (change + applied * (updated - cur_ref[:, span]), total + applied * updated)

            zero = jnp.zeros((comps, TILE), jnp.float32)
            change, total = lax.fori_loop(0, blocks, finish, (zero, zero), unroll=4)
            stat_ref[...] = jnp.zeros_like(stat_ref)
            stat_ref[0:1, :] = jnp.sum(change, axis=0, keepdims=True)
            stat_ref[1:2, :] = jnp.sum(total, axis=0, keepdims=True)


def apply_all(code, sep_idx, sep_count, tile_vals, blend, recv, couple, extras=()):
    tiles = tile_vals.shape[0]
    chunk = code.shape[1]
    comps, nodes = blend.shape
    blocks = nodes // TILE
    _, rounds, slots = sep_idx.shape
    outs = [(comps, nodes), (8, TILE)] if extras else [(comps, nodes)]
    f32 = jnp.float32
    whole = lambda shape: pl.BlockSpec(shape, lambda i, *_: (0,) * len(shape))
    return pl.pallas_call(
        functools.partial(apply_kernel, chunk, bool(extras)),
        out_shape=[jax.ShapeDtypeStruct(o, f32) for o in outs],
        grid_spec=pltpu.PrefetchScalarGridSpec(
            num_scalar_prefetch=3,
            grid=(tiles // chunk,),
            in_specs=[
                pl.BlockSpec((chunk, TILE, TILE), lambda i, *_: (i, 0, 0)),
                whole(blend.shape), whole(recv.shape), whole(couple.shape),
            ] + [whole(e.shape) for e in extras],
            out_specs=[whole(o) for o in outs],
            scratch_shapes=[
                *[pltpu.VMEM((blocks + 1, comps, TILE), f32) for _ in range(BANKS)],
                pltpu.VMEM((nodes, comps), f32),
                pltpu.VMEM((slots, comps), f32),
            ],
        ),
        compiler_params=pltpu.CompilerParams(dimension_semantics=("arbitrary",), vmem_limit_bytes=LIMIT),
        name="apply_all",
    )(code, sep_idx, sep_count, tile_vals, blend, recv, couple, *extras)


def local(rows, cols, factor, prior, tile_src, tile_dst, tile_count, tile_vals, sep_idx, sep_count, couple, masks):
    nodes_all = rows * cols * factor.shape[1]
    smalls = (sep_idx, sep_count, masks)
    tiles, blocks = tile_src.shape[1], factor.shape[1] // TILE
    live = jnp.arange(tiles, dtype=jnp.int32)[None, :] < tile_count[0]
    chunk = 64 if tiles % 64 == 0 else 8
    code = (jnp.where(live, tile_dst, blocks) * (1 << SHIFT) + tile_src).reshape(tiles // chunk, chunk)
    blend, recv = step("first", rows, cols, nodes_all, 0, smalls, (factor, prior))
    current = factor
    for iterate in range(ITERS):
        final = iterate == ITERS - 1
        result = apply_all(code, sep_idx, sep_count, tile_vals, blend, recv, couple[0], (current,) if final else ())
        if not final:
            current, blend, recv = step("middle", rows, cols, nodes_all, 1 + iterate, smalls, (current, blend, *result))
    current, stat = result
    beta, energy = step("last", rows, cols, nodes_all, ITERS, (), (stat,))
    return (current, beta[0, 0], energy[0, 0])


def solution(mesh):
    rows, cols = mesh.shape["row"], mesh.shape["col"]
    in_specs = (
        P(None, ("row", "col")),
        P(None, ("row", "col")),
        P(("row", "col"), None),
        P(("row", "col"), None),
        P(("row", "col")),
        P(("row", "col"), None, None),
        P(("row", "col"), None, None),
        P(("row", "col"), None),
        P(("row", "col"), None, None, None),
        P(),
    )
    out_specs = (P(None, ("row", "col")), P(), P())
    return jax.shard_map(functools.partial(local, rows, cols), mesh=mesh, in_specs=in_specs, out_specs=out_specs, check_vma=False)
```

profile of v0, /device:TPU:0, one launch (start us, length us, event | category | flops | bytes accessed | tf_op | source)
XLA Modules:
  0.0 77.8 jit_solution(5661671580235492063)
XLA Ops:
  1.3 0.7 fusion.2
  2.0 0.7 reshape.17.code_ref
  2.7 16.8 %step_first.1 = (f32[24,8192]{1,0:T(8,128)}, bf16[4,24,256]{2,1,0:T(8,128)(2,1)}) custom-call(s32[1,4,256]{2,1,0:T(4,128)} %idx_ref.3, s32[1,4]{1,0:T(1,128)} %cnt_ref.3, s32[4]{0:T(128)} %refs_2_.3, f32[24,8192]{1,0:T(8,128)} %refs_3_.3, f32[24,8192]{1,0:T(8,128)} %refs_4_.1), custom_call_target="tpu_custom_call" | custom-call | tf_op jit(solution)/shard_map/step_first/pallas_call | solution.py:258
  19.5 13.0 %apply_all.2.refs_5_ = f32[24,8192]{1,0:T(8,128)} custom-call(s32[6,64]{1,0:T(8,128)} %reshape.17.code_ref, s32[1,4,256]{2,1,0:T(4,128)} %idx_ref.3, s32[1,4]{1,0:T(1,128)} %cnt_ref.3, bf16[384,128,128]{2,1,0:T(8,128)(2,1)} %vals_ref.3, f32[24,8192]{1,0:T(8,128)} %get-tuple-element.12.blend_ref.refs_4_, bf16[4,24,256]{2,1,0:T(8,128)(2,1)} %get-tuple-element.13.recv_ref, ...), custom_call_target="tpu_custom_call" | custom-call | tf_op jit(solution)/shard_map/apply_all/pallas_call | solution.py:345
  32.4 17.6 %step_middle.1 = (f32[24,8192]{1,0:T(8,128)}, f32[24,8192]{1,0:T(8,128)}, bf16[4,24,256]{2,1,0:T(8,128)(2,1)}) custom-call(s32[1,4,256]{2,1,0:T(4,128)} %idx_ref.3, s32[1,4]{1,0:T(1,128)} %cnt_ref.3, s32[4]{0:T(128)} %refs_2_.3, f32[24,8192]{1,0:T(8,128)} %refs_3_.3, f32[24,8192]{1,0:T(8,128)} %get-tuple-element.12.blend_ref.refs_4_, ...), custom_call_target="tpu_custom_call" | custom-call | tf_op jit(solution)/shard_map/step_middle/pallas_call | solution.py:258
  50.1 13.7 %apply_all.3 = (f32[24,8192]{1,0:T(8,128)}, f32[8,128]{1,0:T(8,128)}) custom-call(s32[6,64]{1,0:T(8,128)} %reshape.17.code_ref, s32[1,4,256]{2,1,0:T(4,128)} %idx_ref.3, s32[1,4]{1,0:T(1,128)} %cnt_ref.3, bf16[384,128,128]{2,1,0:T(8,128)(2,1)} %vals_ref.3, f32[24,8192]{1,0:T(8,128)} %get-tuple-element.14.blend_ref, ...), custom_call_target="tpu_custom_call" | custom-call | tf_op jit(solution)/shard_map/apply_all/pallas_call | solution.py:345
  63.8 10.5 %step_last.1 = (f32[1,128]{1,0:T(1,128)}, f32[1,128]{1,0:T(1,128)}) custom-call(f32[8,128]{1,0:T(8,128)} %get-tuple-element.18.refs_0_), custom_call_target="tpu_custom_call" | custom-call | tf_op jit(solution)/shard_map/step_last/pallas_call | solution.py:258
where the time goes:
time: 78.3 us; the launch traced here: 77.8 us
  Pallas kernels  71.6 us (91%)
  between operations  4.82 us (6%)
    pallas_call x3, Pallas kernels, step(): pl.pallas_call(functools.partial(step_kernel, mode, rows, cols, nodes_all...  44.9 us
    pallas_call x2, Pallas kernels, apply_all(): pl.pallas_call(functools.partial(apply_kernel, chunk, bool(extras)), out_...  26.7 us

commit v1 on v0

v1 whole, which is shorter than its diff:
```python
import functools

import jax
import jax.numpy as jnp
from jax import lax
from jax.experimental import pallas as pl
from jax.experimental.pallas import tpu as pltpu
from jax.sharding import PartitionSpec as P

TILE = 128
WIDE = 2 * TILE
MOMENTUM_CAP = 0.9
MESH = pl.DeviceIdType.MESH
LIMIT = 60 * 1024 * 1024
UNROLL = 16
SPLIT = 2
GROUP = 8
PIECES = 8


def flip(x, j):
    bit = 1
    while bit <= j:
        if j & bit:
            x = x + bit * (1 - 2 * ((x // bit) % 2))
        bit *= 2
    return x


def above(n):
    return 1 << (n - 1).bit_length()


def kernel(rows, cols, nodes_all, *refs):
    refs = list(refs)
    take = lambda n: [refs.pop(0) for _ in range(n)]
    fac_h, pri_h, src_h, dst_h, live_h, vals_h, idx_h, cnt_h, cpl_h, masks_h = take(10)
    out_h, beta_ref, energy_ref = take(3)
    fac, pri, src, dst, live, vals, idx, cnt, cpl, masks = take(10)
    code_v, loc_v, code, loc, lt = take(5)
    blend3, upd3, app3, both16, pack, run1, run2 = take(7)
    sbuf, direct, picked, stat = take(4)
    bcol, brow = take(3), take(3)
    in_sem, vals_sem, table_sem, out_sem = take(4)
    d_send, d_recv, c_send, c_recv, r_send, r_recv, st_send, st_recv = take(8)

    parts = rows * cols
    comps, nodes = fac.shape
    blocks = nodes // TILE
    supers = nodes // WIDE
    tiles = vals.shape[0]
    rounds, slots = idx.shape
    f32, bf16 = jnp.float32, jnp.bfloat16
    r = lax.axis_index("row")
    c = lax.axis_index("col")

    barrier = pltpu.get_barrier_semaphore()
    everyone = [(jr, jc) for jr in range(rows) for jc in range(cols) if jr or jc]
    for jr, jc in everyone:
        pl.semaphore_signal(barrier, inc=1, device_id=(flip(r, jr), flip(c, jc)), device_id_type=MESH)

    pairs = [(idx_h.at[0], idx), (fac_h, fac), (pri_h, pri), (cnt_h, cnt), (src_h, src), (dst_h, dst), (live_h, live),
             (masks_h, masks), (cpl_h.at[0], cpl)]
    loads = [pltpu.make_async_copy(a, b, in_sem.at[i]) for i, (a, b) in enumerate(pairs)]
    piece = tiles // PIECES
    spans = [pl.ds(i * piece, piece) for i in range(PIECES)]
    vals_loads = [pltpu.make_async_copy(vals_h.at[s], vals.at[s], vals_sem.at[i]) for i, s in enumerate(spans)]
    for copy in loads + vals_loads:
        copy.start()

    def lanes(b):
        return pl.ds(pl.multiple_of(b * TILE, TILE), TILE)

    slot_range = lax.broadcasted_iota(jnp.int32, (comps, slots), 1)
    loads[0].wait()
    lane_range = lax.broadcasted_iota(jnp.int32, (WIDE, slots), 0)
    for k in range(rounds):
        lt[k] = jnp.where(lane_range == (idx[k:k + 1, :] & (WIDE - 1)), 1.0, 0.0).astype(bf16)

    def home(k):
        return jnp.broadcast_to(idx[k:k + 1, :] // WIDE, (comps, slots))

    beta0 = 0.5 * MOMENTUM_CAP
    loads[1].wait()
    loads[2].wait()
    span4 = 2 * WIDE

    def doubled(x):
        return jnp.concatenate([x[:, :WIDE], x[:, WIDE:]], axis=0).astype(bf16)

    def begin(q, carry):
        at = pl.ds(pl.multiple_of(q * span4, span4), span4)
        f = fac[:, at]
        b = f + beta0 * (f - pri[:, at])
        pack[0, q] = doubled(b)
        pack[1, q] = doubled(f)
        for i in range(4):
            part = slice(i * TILE, (i + 1) * TILE)
            blend3[4 * q + i] = b[:, part]
            both16[4 * q + i] = jnp.concatenate([b[:, part], f[:, part]], axis=0).astype(bf16)
        return carry

    lax.fori_loop(0, supers // 2, begin, 0, unroll=2)
    loads[3].wait()

    def fixed(k):
        if k == 0:
            return parts - 1
        if k == 1:
            return parts // 2
        return 1 if k == rounds - 1 else None

    loose = [k for k in range(rounds) if fixed(k) is None]
    firm = [k for k in range(rounds) if fixed(k) is not None]

    def gather(kind, k):
        one = lt[k]
        where = home(k)
        total = jnp.zeros((comps, slots), f32)
        step = GROUP // 2
        for q in range(0, supers // 2, step):
            rows_in = pack[kind, q:q + step].reshape(step * 2 * comps, WIDE)
            got = jnp.dot(rows_in, one, preferred_element_type=f32)
            for i in range(GROUP):
                total = jnp.where(where == 2 * q + i, got[i * comps:(i + 1) * comps], total)
        sbuf[kind, k] = jnp.where(slot_range < cnt[0, k], total, 0.0).astype(bf16)

    started = []

    def go(copy):
        copy.start()
        started.append(copy)

    def direct_copy(kind, k):
        mask = fixed(k)
        return pltpu.make_async_remote_copy(
            src_ref=sbuf.at[kind, k], dst_ref=direct.at[kind, k], send_sem=d_send.at[kind, k], recv_sem=d_recv.at[kind, k],
            device_id=(flip(r, mask // cols), flip(c, mask % cols)), device_id_type=MESH)

    def col_copy(kind, n, j):
        return pltpu.make_async_remote_copy(
            src_ref=sbuf.at[kind, loose[n]], dst_ref=bcol[kind].at[n, j], send_sem=c_send.at[kind, n, j],
            recv_sem=c_recv.at[kind, n, j], device_id=(r, flip(c, j)), device_id_type=MESH)

    def row_copy(kind, n, j):
        return pltpu.make_async_remote_copy(
            src_ref=picked.at[kind, n], dst_ref=brow[kind].at[n, j], send_sem=r_send.at[kind, n, j],
            recv_sem=r_recv.at[kind, n, j], device_id=(flip(r, j), c), device_id_type=MESH)

    def send_loose(kind):
        for n in range(len(loose)):
            for j in range(cols - 1, 0, -1):
                go(col_copy(kind, n, j))
            bcol[kind][n, 0] = sbuf[kind, loose[n]]

    def relay(kind):
        for n, k in enumerate(loose):
            for j in range(1, cols):
                col_copy(kind, n, j).wait_recv()
            picked[kind, n] = bcol[kind][n, masks[k] % cols]
            for j in range(rows - 1, 0, -1):
                go(row_copy(kind, n, j))
            brow[kind][n, 0] = picked[kind, n]

    def take_loose(kind, n):
        for j in range(1, rows):
            row_copy(kind, n, j).wait_recv()
        return brow[kind][n, masks[loose[n]] // cols]

    def take_firm(kind, k):
        direct_copy(kind, k).wait_recv()
        return direct[kind, k]

    def send_firm(kind):
        for k in firm:
            go(direct_copy(kind, k))

    def stat_copy(stage, jr, jc):
        j = jr * cols + jc
        return pltpu.make_async_remote_copy(
            src_ref=stat.at[stage, 0], dst_ref=stat.at[stage, j], send_sem=st_send.at[stage, j], recv_sem=st_recv.at[stage, j],
            device_id=(flip(r, jr), flip(c, jc)), device_id_type=MESH)

    def stat_send(stage, change, total):
        half = lax.broadcasted_iota(jnp.int32, (1, TILE), 1) < TILE // 2
        fold = lambda x: x + pltpu.roll(x, TILE // 2, 1)
        change = fold(jnp.sum(change, axis=0, keepdims=True))
        total = fold(jnp.sum(total, axis=0, keepdims=True))
        stat[stage, 0] = jnp.where(half, change, total)
        for jr, jc in reversed(everyone):
            go(stat_copy(stage, jr, jc))

    def stat_take(stage):
        for jr, jc in everyone:
            stat_copy(stage, jr, jc).wait_recv()
        every = [stat[stage, j] for j in range(parts)]
        while len(every) > 1:
            every = [every[i] + every[i + 1] for i in range(0, len(every), 2)]
        half = lax.broadcasted_iota(jnp.int32, (1, TILE), 1) < TILE // 2
        sums = every[0] / nodes_all
        change = jnp.sum(jnp.where(half, sums, 0.0), axis=1, keepdims=True)
        energy = jnp.sum(jnp.where(half, 0.0, sums), axis=1, keepdims=True)
        return MOMENTUM_CAP * 0.5 * (1.0 + jnp.tanh(change)), energy

    for k in loose:
        gather(0, k)
    for copy in loads[4:7]:
        copy.wait()
    tile_row = lax.broadcasted_iota(jnp.int32, (1, tiles), 1)
    room = above(tiles)
    inner = above(blocks)
    key = jnp.where(tile_row < live[0], dst[...], blocks)
    rank_key = key * room + tile_row
    packed_code = (key * inner + src[...]) * room + tile_row

    def upright(x):
        return jnp.broadcast_to(x, (8, tiles)).T[:, :1]

    count = lambda mask: jnp.sum(jnp.where(mask, 1, 0), axis=0, keepdims=True)
    rank = count(upright(rank_key) < rank_key)
    code_col = upright(packed_code)
    code_v[...] = jnp.sum(jnp.where(upright(rank) == tile_row, code_col, 0), axis=0, keepdims=True)
    key_col = code_col // (inner * room)
    block_row = lax.broadcasted_iota(jnp.int32, loc_v.shape, 1)
    loc_v[...] = jnp.where(count(key_col == block_row) > 0, count(key_col <= block_row) - 1, tiles)
    tables = [pltpu.make_async_copy(code_v, code, table_sem.at[0]), pltpu.make_async_copy(loc_v, loc, table_sem.at[1])]
    for copy in tables:
        copy.start()
    loads[7].wait()
    pl.semaphore_wait(barrier, len(everyone))
    send_loose(0)
    for k in firm:
        gather(0, k)
    send_firm(0)
    for k in loose + firm:
        gather(1, k)
    run1[tiles] = jnp.zeros((2 * comps, TILE), f32)
    run2[tiles] = jnp.zeros((comps, TILE), f32)
    for copy in tables + vals_loads:
        copy.wait()

    def run_tiles(run, source, start, stop, carry):
        def some(i, carry):
            acc, last = carry
            base = i * UNROLL
            for j in range(0, UNROLL, 2):
                codes = [code[0, base + j + h] for h in range(2)]
                keys = [v // (inner * room) for v in codes]
                x = jnp.concatenate([source((v // room) % inner) for v in codes], axis=0).astype(bf16)
                side = jnp.concatenate([vals[v % room] for v in codes], axis=1)
                got = jnp.dot(x, side, preferred_element_type=f32)
                n = x.shape[0] // 2
                for h in range(2):
                    acc = jnp.where(keys[h] == last, acc, 0.0) + got[h * n:(h + 1) * n, h * TILE:(h + 1) * TILE]
                    run[base + j + h] = acc
                    last = keys[h]
            return acc, last

        return lax.fori_loop(start, stop, some, carry)

    steps = tiles // UNROLL
    middle = steps // SPLIT
    carry = (jnp.zeros((2 * comps, TILE), f32), jnp.int32(-1))
    carry = run_tiles(run1, lambda s: both16[s], 0, middle, carry)
    relay(0)
    send_loose(1)
    send_firm(1)
    run_tiles(run1, lambda s: both16[s], middle, steps, carry)
    loads[8].wait()

    def extra(k, received):
        e = jnp.dot(received, cpl[k], preferred_element_type=f32)
        return jnp.where(slot_range < cnt[0, k], e, 0.0)

    def scatter(first, found):
        total = None
        for k, e in found:
            where = home(k)
            left = jnp.concatenate([jnp.where(where == first + i, e, 0.0) for i in range(GROUP)], axis=0).astype(bf16)
            got = lax.dot_general(left, lt[k], (((1,), (1,)), ((), ())), preferred_element_type=f32)
            total = got if total is None else total + got
        return lambda i: total[(i // 2) * comps:(i // 2 + 1) * comps, (i % 2) * TILE:(i % 2 + 1) * TILE]

    group_blocks = 2 * GROUP

    def partial(found, product):
        for g in range(0, supers, GROUP):
            at = scatter(g, found)
            for i in range(group_blocks):
                b = 2 * g + i
                app3[b] = product(b) + at(i)

    def finish(found, blend, old, keep, after):
        zero = jnp.zeros((comps, TILE), f32)
        change, total = zero, zero
        for g in range(0, supers, GROUP):
            at = scatter(g, found)
            news = []
            for i in range(group_blocks):
                b = 2 * g + i
                applied = app3[b] + at(i)
                moved = blend(b) + applied
                scale = lax.rsqrt(jnp.maximum(jnp.sum(moved * moved, axis=0, keepdims=True), 1.0))
                updated = moved * scale
                keep(b, updated)
                news.append(updated)
                change = change + applied * (updated - old(b))
                total = total + applied * updated
            after(g, news)
        return change, total

    old0 = lambda b: fac[:, b * TILE:(b + 1) * TILE]
    partial([(k, extra(k, take_firm(0, k))) for k in firm], lambda b: run1[loc[0, b], :comps])
    found = [(k, extra(k, take_loose(0, n))) for n, k in enumerate(loose)]

    def keep_upd(b, updated):
        upd3[b] = updated

    def pack_upd(g, news):
        for i in range(0, len(news), 4):
            pack[2, g // 2 + i // 4] = doubled(jnp.concatenate(news[i:i + 4], axis=1))

    change, total = finish(found, lambda b: blend3[b], old0, keep_upd, pack_upd)
    stat_send(0, change, total)

    for k in loose:
        gather(2, k)
    send_loose(2)
    for k in firm:
        gather(2, k)
    send_firm(2)
    carry = (jnp.zeros((comps, TILE), f32), jnp.int32(-1))
    run_tiles(run2, lambda s: upd3[s], 0, steps, carry)
    relay(1)
    relay(2)
    beta, _ = stat_take(0)

    def mix(new, old):
        return (1.0 + beta) * new - beta * old

    def mixed(get, k):
        return mix(get(2, k).astype(f32), get(1, k).astype(f32)).astype(bf16)

    partial([(k, extra(k, mixed(take_firm, k))) for k in firm],
            lambda b: mix(run2[loc[0, b]], run1[loc[0, b], comps:]))
    found = [(k, extra(k, mixed(take_loose, n))) for n, k in enumerate(loose)]
    outs = []

    def keep_out(b, updated):
        pri[:, b * TILE:(b + 1) * TILE] = updated

    def write_out(g, news):
        span = pl.ds(g * WIDE, GROUP * WIDE)
        copy = pltpu.make_async_copy(pri.at[:, span], out_h.at[:, span], out_sem.at[g // GROUP])
        copy.start()
        outs.append(copy)

    change, total = finish(found, lambda b: upd3[b] + beta * (upd3[b] - old0(b)), lambda b: upd3[b], keep_out, write_out)
    stat_send(1, change, total)
    beta, energy = stat_take(1)
    beta_ref[...] = jnp.broadcast_to(beta, beta_ref.shape)
    energy_ref[...] = jnp.broadcast_to(energy, energy_ref.shape)
    for copy in outs:
        copy.wait()
    for copy in started:
        copy.wait_send()


def local(rows, cols, factor, prior, tile_src, tile_dst, tile_count, tile_vals, sep_idx, sep_count, couple, masks):
    comps, nodes = factor.shape
    tiles = tile_src.shape[1]
    blocks = nodes // TILE
    supers = nodes // WIDE
    _, rounds, slots = sep_idx.shape
    parts = rows * cols
    loose = max(rounds - 3, 1)
    f32, bf16, i32 = jnp.float32, jnp.bfloat16, jnp.int32
    vm, sm, dma = pltpu.VMEM, pltpu.SMEM, pltpu.SemaphoreType.DMA
    table = -(-blocks // TILE) * TILE
    args = (factor, prior, tile_src, tile_dst, tile_count, tile_vals, sep_idx, sep_count, couple, masks)
    result, beta, energy = pl.pallas_call(
        functools.partial(kernel, rows, cols, nodes * parts),
        out_shape=[jax.ShapeDtypeStruct((comps, nodes), f32)] + [jax.ShapeDtypeStruct((1, TILE), f32)] * 2,
        in_specs=[pl.BlockSpec(memory_space=pl.ANY)] * len(args),
        out_specs=[pl.BlockSpec(memory_space=pl.ANY)] + [pl.BlockSpec(memory_space=pltpu.VMEM)] * 2,
        scratch_shapes=[
            vm((comps, nodes), f32), vm((comps, nodes), f32), vm((1, tiles), i32), vm((1, tiles), i32), sm((1,), i32),
            vm(tile_vals.shape, bf16), vm((rounds, slots), i32), sm((1, rounds), i32), vm((rounds, slots, slots), bf16), sm((rounds,), i32),
            vm((1, tiles), i32), vm((1, table), i32), sm((1, tiles), i32), sm((1, table), i32), vm((rounds, WIDE, slots), bf16),
            vm((blocks, comps, TILE), f32), vm((blocks, comps, TILE), f32), vm((blocks, comps, TILE), f32),
            vm((blocks, 2 * comps, TILE), bf16), vm((3, supers // 2, 2 * comps, WIDE), bf16),
            vm((tiles + 1, 2 * comps, TILE), f32), vm((tiles + 1, comps, TILE), f32),
            vm((3, rounds, comps, slots), bf16), vm((3, rounds, comps, slots), bf16),
            vm((3, loose, comps, slots), bf16), vm((2, parts, 1, TILE), f32),
            *[vm((loose, cols, comps, slots), bf16)] * 3, *[vm((loose, rows, comps, slots), bf16)] * 3,
            dma((9,)), dma((PIECES,)), dma((2,)), dma((supers // GROUP,)),
            dma((3, rounds)), dma((3, rounds)), dma((3, loose, cols)), dma((3, loose, cols)), dma((3, loose, rows)), dma((3, loose, rows)),
            dma((2, parts)), dma((2, parts)),
        ],
        compiler_params=pltpu.CompilerParams(collective_id=0, has_side_effects=True, vmem_limit_bytes=LIMIT),
        name="rounds",
    )(*args)
    return result, beta[0, 0], energy[0, 0]


def solution(mesh):
    rows, cols = mesh.shape["row"], mesh.shape["col"]
    whole = P(("row", "col"))
    in_specs = (
        P(None, ("row", "col")), P(None, ("row", "col")),
        P(("row", "col"), None), P(("row", "col"), None), whole,
        P(("row", "col"), None, None), P(("row", "col"), None, None), P(("row", "col"), None),
        P(("row", "col"), None, None, None), P(),
    )
    out_specs = (P(None, ("row", "col")), P(), P())
    return jax.shard_map(functools.partial(local, rows, cols), mesh=mesh, in_specs=in_specs, out_specs=out_specs, check_vma=False)
```

time: 78.3 us -> 44.6 us (0.57)
  Pallas kernels: 71.6 us -> 37.6 us
  local copies, waits for them, and re-layouts: 0.67 us -> 2.06 us
    pallas_call x5 -> x1, Pallas kernels: 71.6 us -> 37.6 us  [local(): pl.pallas_call(functools.partial(kernel, rows, cols, nodes * parts), out_...]
    unnamed x0 -> x1, local copies, waits for them, and re-layouts: none -> 2.06 us
where the time goes in v1:
time: 44.6 us; the launch traced here: 44.4 us
  Pallas kernels  37.6 us (84%)
  between operations  4.73 us (11%)
  local copies, waits for them, and re-layouts  2.06 us (5%)
    pallas_call x1, Pallas kernels, local(): pl.pallas_call(functools.partial(kernel, rows, cols, nodes * parts), out_...  37.6 us
    unnamed x1, local copies, waits for them, and re-layouts  2.06 us

profile of v1, /device:TPU:0, one launch (start us, length us, event | category | flops | bytes accessed | tf_op | source)
XLA Modules:
  0.0 44.4 jit_solution(5550641588490492835)
XLA Ops:
  1.3 37.6 %rounds.1 = (f32[24,8192]{1,0:T(8,128)}, f32[1,128]{1,0:T(1,128)}, f32[1,128]{1,0:T(1,128)}) custom-call(f32[24,8192]{1,0:T(8,128)} %refs_0_.1, f32[24,8192]{1,0:T(8,128)} %refs_1_.1, s32[1,384]{1,0:T(1,128)} %refs_2_.1, s32[1,384]{1,0:T(1,128)} %refs_3_.1, s32[1]{0:T(128)S(6)} %copy.16.refs_4_, bf16[384,128,128]{2,1,0:T(8,128)(2,1)} %refs_5_.1, ...), custom_call_target="tpu_custom_call" | custom-call | tf_op jit(solution)/shard_map/rounds/pallas_call | solution.py:381
  38.9 2.1 %copy.17 = f32[24,8192]{1,0:T(8,128)} copy(f32[24,8192]{1,0:T(8,128)} %get-tuple-element.12) | data formatting | bytes 1572864

commit v2 on v1

--- a/solution.py
+++ b/solution.py
@@ -11,11 +11,10 @@
 WIDE = 2 * TILE
 MOMENTUM_CAP = 0.9
 MESH = pl.DeviceIdType.MESH
-LIMIT = 60 * 1024 * 1024
-UNROLL = 16
-SPLIT = 2
+LIMIT = 48 * 1024 * 1024
+UNROLL = 32
+SPLIT = (3, 4)
 GROUP = 8
-PIECES = 8
 
 
 def flip(x, j):
@@ -37,11 +36,11 @@
     fac_h, pri_h, src_h, dst_h, live_h, vals_h, idx_h, cnt_h, cpl_h, masks_h = take(10)
     out_h, beta_ref, energy_ref = take(3)
     fac, pri, src, dst, live, vals, idx, cnt, cpl, masks = take(10)
-    code_v, loc_v, code, loc, lt = take(5)
+    order_v, loc_v, order, loc, lt = take(5)
     blend3, upd3, app3, both16, pack, run1, run2 = take(7)
     sbuf, direct, picked, stat = take(4)
     bcol, brow = take(3), take(3)
-    in_sem, vals_sem, table_sem, out_sem = take(4)
+    in_sem, table_sem, out_sem = take(3)
     d_send, d_recv, c_send, c_recv, r_send, r_recv, st_send, st_recv = take(8)
 
     parts = rows * cols
@@ -62,10 +61,8 @@
     pairs = [(idx_h.at[0], idx), (fac_h, fac), (pri_h, pri), (cnt_h, cnt), (src_h, src), (dst_h, dst), (live_h, live),
              (masks_h, masks), (cpl_h.at[0], cpl)]
     loads = [pltpu.make_async_copy(a, b, in_sem.at[i]) for i, (a, b) in enumerate(pairs)]
-    piece = tiles // PIECES
-    spans = [pl.ds(i * piece, piece) for i in range(PIECES)]
-    vals_loads = [pltpu.make_async_copy(vals_h.at[s], vals.at[s], vals_sem.at[i]) for i, s in enumerate(spans)]
-    for copy in loads + vals_loads:
+    loads.append(pltpu.make_async_copy(vals_h, vals, in_sem.at[len(pairs)]))
+    for copy in loads:
         copy.start()
 
     def lanes(b):
@@ -125,61 +122,57 @@
                 total = jnp.where(where == 2 * q + i, got[i * comps:(i + 1) * comps], total)
         sbuf[kind, k] = jnp.where(slot_range < cnt[0, k], total, 0.0).astype(bf16)
 
-    started = []
-
-    def go(copy):
-        copy.start()
-        started.append(copy)
-
-    def direct_copy(kind, k):
-        mask = fixed(k)
+    pending = []
+
+    def remote(source, target, send_sem, recv_sem, place):
         return pltpu.make_async_remote_copy(
-            src_ref=sbuf.at[kind, k], dst_ref=direct.at[kind, k], send_sem=d_send.at[kind, k], recv_sem=d_recv.at[kind, k],
-            device_id=(flip(r, mask // cols), flip(c, mask % cols)), device_id_type=MESH)
-
-    def col_copy(kind, n, j):
-        return pltpu.make_async_remote_copy(
-            src_ref=sbuf.at[kind, loose[n]], dst_ref=bcol[kind].at[n, j], send_sem=c_send.at[kind, n, j],
-            recv_sem=c_recv.at[kind, n, j], device_id=(r, flip(c, j)), device_id_type=MESH)
-
-    def row_copy(kind, n, j):
-        return pltpu.make_async_remote_copy(
-            src_ref=picked.at[kind, n], dst_ref=brow[kind].at[n, j], send_sem=r_send.at[kind, n, j],
-            recv_sem=r_recv.at[kind, n, j], device_id=(flip(r, j), c), device_id_type=MESH)
+            src_ref=source, dst_ref=target, send_sem=send_sem, recv_sem=recv_sem, device_id=place, device_id_type=MESH)
+
+    def whole(target, send_sem, recv_sem):
+        return remote(target, target, send_sem, recv_sem, (flip(r, 1), c))
+
+    def firm_whole(kind):
+        return whole(direct.at[kind], d_send.at[kind], d_recv.at[kind])
+
+    def send_firm(kind):
+        for m, k in enumerate(firm):
+            place = (flip(r, fixed(k) // cols), flip(c, fixed(k) % cols))
+            remote(sbuf.at[kind, k], direct.at[kind, m], d_send.at[kind], d_recv.at[kind], place).start()
+        pending.append(firm_whole(kind))
+
+    def col_whole(kind, n):
+        return whole(bcol[kind].at[n, pl.ds(1, cols - 1)], c_send.at[kind, n], c_recv.at[kind, n])
+
+    def row_whole(kind, n):
+        return whole(brow[kind].at[n, pl.ds(1, rows - 1)], r_send.at[kind, n], r_recv.at[kind, n])
 
     def send_loose(kind):
-        for n in range(len(loose)):
+        for n, k in enumerate(loose):
             for j in range(cols - 1, 0, -1):
-                go(col_copy(kind, n, j))
-            bcol[kind][n, 0] = sbuf[kind, loose[n]]
+                remote(sbuf.at[kind, k], bcol[kind].at[n, j], c_send.at[kind, n], c_recv.at[kind, n], (r, flip(c, j))).start()
+            pending.append(col_whole(kind, n))
+            bcol[kind][n, 0] = sbuf[kind, k]
 
     def relay(kind):
         for n, k in enumerate(loose):
-            for j in range(1, cols):
-                col_copy(kind, n, j).wait_recv()
-            picked[kind, n] = bcol[kind][n, masks[k] % cols]
+            col_whole(kind, n).wait_recv()
+            picked[kind, n] = bcol[kind][n, masks[0, k] % cols]
             for j in range(rows - 1, 0, -1):
-                go(row_copy(kind, n, j))
+                remote(picked.at[kind, n], brow[kind].at[n, j], r_send.at[kind, n], r_recv.at[kind, n], (flip(r, j), c)).start()
+            pending.append(row_whole(kind, n))
             brow[kind][n, 0] = picked[kind, n]
 
-    def take_loose(kind, n):
-        for j in range(1, rows):
-            row_copy(kind, n, j).wait_recv()
-        return brow[kind][n, masks[loose[n]] // cols]
-
-    def take_firm(kind, k):
-        direct_copy(kind, k).wait_recv()
-        return direct[kind, k]
-
-    def send_firm(kind):
-        for k in firm:
-            go(direct_copy(kind, k))
-
-    def stat_copy(stage, jr, jc):
-        j = jr * cols + jc
-        return pltpu.make_async_remote_copy(
-            src_ref=stat.at[stage, 0], dst_ref=stat.at[stage, j], send_sem=st_send.at[stage, j], recv_sem=st_recv.at[stage, j],
-            device_id=(flip(r, jr), flip(c, jc)), device_id_type=MESH)
+    def take_loose(kind):
+        for n in range(len(loose)):
+            row_whole(kind, n).wait_recv()
+        return {k: brow[kind][n, masks[0, k] // cols] for n, k in enumerate(loose)}
+
+    def take_firm(kind):
+        firm_whole(kind).wait_recv()
+        return {k: direct[kind, m] for m, k in enumerate(firm)}
+
+    def stat_whole(stage):
+        return whole(stat.at[stage, pl.ds(1, parts - 1)], st_send.at[stage], st_recv.at[stage])
 
     def stat_send(stage, change, total):
         half = lax.broadcasted_iota(jnp.int32, (1, TILE), 1) < TILE // 2
@@ -188,11 +181,11 @@
         total = fold(jnp.sum(total, axis=0, keepdims=True))
         stat[stage, 0] = jnp.where(half, change, total)
         for jr, jc in reversed(everyone):
-            go(stat_copy(stage, jr, jc))
+            remote(stat.at[stage, 0], stat.at[stage, jr * cols + jc], st_send.at[stage], st_recv.at[stage], (flip(r, jr), flip(c, jc))).start()
+        pending.append(stat_whole(stage))
 
     def stat_take(stage):
-        for jr, jc in everyone:
-            stat_copy(stage, jr, jc).wait_recv()
+        stat_whole(stage).wait_recv()
         every = [stat[stage, j] for j in range(parts)]
         while len(every) > 1:
             every = [every[i] + every[i + 1] for i in range(0, len(every), 2)]
@@ -204,63 +197,62 @@
 
     for k in loose:
         gather(0, k)
-    for copy in loads[4:7]:
-        copy.wait()
-    tile_row = lax.broadcasted_iota(jnp.int32, (1, tiles), 1)
-    room = above(tiles)
-    inner = above(blocks)
-    key = jnp.where(tile_row < live[0], dst[...], blocks)
-    rank_key = key * room + tile_row
-    packed_code = (key * inner + src[...]) * room + tile_row
-
-    def upright(x):
-        return jnp.broadcast_to(x, (8, tiles)).T[:, :1]
-
-    count = lambda mask: jnp.sum(jnp.where(mask, 1, 0), axis=0, keepdims=True)
-    rank = count(upright(rank_key) < rank_key)
-    code_col = upright(packed_code)
-    code_v[...] = jnp.sum(jnp.where(upright(rank) == tile_row, code_col, 0), axis=0, keepdims=True)
-    key_col = code_col // (inner * room)
-    block_row = lax.broadcasted_iota(jnp.int32, loc_v.shape, 1)
-    loc_v[...] = jnp.where(count(key_col == block_row) > 0, count(key_col <= block_row) - 1, tiles)
-    tables = [pltpu.make_async_copy(code_v, code, table_sem.at[0]), pltpu.make_async_copy(loc_v, loc, table_sem.at[1])]
-    for copy in tables:
-        copy.start()
     loads[7].wait()
     pl.semaphore_wait(barrier, len(everyone))
     send_loose(0)
     for k in firm:
         gather(0, k)
     send_firm(0)
+    for copy in loads[4:7]:
+        copy.wait()
+    tile_row = lax.broadcasted_iota(jnp.int32, (1, tiles), 1)
+    key = jnp.where(tile_row < live[0], dst[...], blocks)
+    ones = lambda mask: jnp.where(mask, 1.0, 0.0)
+    across = lambda a, b: lax.dot_general(a.astype(bf16), b.astype(bf16), (((1,), (1,)), ((), ())), preferred_element_type=f32)
+    block_at = lax.broadcasted_iota(jnp.int32, (loc_v.shape[1], tiles), 0)
+    same = ones(block_at == key)
+    upto = ones(key <= block_at)
+    left = lax.broadcasted_iota(jnp.int32, (tiles, tiles), 0)
+    ahead = jnp.dot(same.astype(bf16), ones(left < tile_row).astype(bf16), preferred_element_type=f32)
+    ends = jnp.sum(upto, axis=1, keepdims=True) - jnp.sum(same, axis=1, keepdims=True)
+    rank = jnp.sum(same * (ahead + ends), axis=0, keepdims=True).astype(jnp.int32)
+    columns = jnp.concatenate([tile_row // TILE, tile_row % TILE, src[...], key] + [tile_row] * 4, axis=0)
+    sort = across(columns.astype(f32), ones(left == rank)).astype(jnp.int32)
+    within = lambda x, n: jnp.minimum(jnp.maximum(x, 0), n)
+    order_v[0:1, :] = within(sort[0:1] * TILE + sort[1:2], tiles - 1)
+    order_v[1:2, :] = within(sort[2:3], blocks - 1)
+    order_v[2:3, :] = jnp.where(sort[3:4] == pltpu.roll(sort, 1, 1)[3:4], 1, 0)
+    unit = jnp.ones((8, tiles), f32)
+    found_at = jnp.where(across(unit, same)[:1] > 0.0, across(unit, upto)[:1].astype(jnp.int32) - 1, tiles)
+    loc_v[...] = within(found_at, tiles)
+    tables = [pltpu.make_async_copy(order_v, order, table_sem.at[0]), pltpu.make_async_copy(loc_v, loc, table_sem.at[1])]
+    for copy in tables:
+        copy.start()
     for k in loose + firm:
         gather(1, k)
     run1[tiles] = jnp.zeros((2 * comps, TILE), f32)
     run2[tiles] = jnp.zeros((comps, TILE), f32)
-    for copy in tables + vals_loads:
+    for copy in tables + loads[9:]:
         copy.wait()
 
     def run_tiles(run, source, start, stop, carry):
         def some(i, carry):
-            acc, last = carry
             base = i * UNROLL
             for j in range(0, UNROLL, 2):
-                codes = [code[0, base + j + h] for h in range(2)]
-                keys = [v // (inner * room) for v in codes]
-                x = jnp.concatenate([source((v // room) % inner) for v in codes], axis=0).astype(bf16)
-                side = jnp.concatenate([vals[v % room] for v in codes], axis=1)
+                x = jnp.concatenate([source(order[1, base + j + h]) for h in range(2)], axis=0).astype(bf16)
+                side = jnp.concatenate([vals[order[0, base + j + h]] for h in range(2)], axis=1)
                 got = jnp.dot(x, side, preferred_element_type=f32)
                 n = x.shape[0] // 2
                 for h in range(2):
-                    acc = jnp.where(keys[h] == last, acc, 0.0) + got[h * n:(h + 1) * n, h * TILE:(h + 1) * TILE]
-                    run[base + j + h] = acc
-                    last = keys[h]
-            return acc, last
+                    carry = jnp.where(order[2, base + j + h] > 0, carry, 0.0) + got[h * n:(h + 1) * n, h * TILE:(h + 1) * TILE]
+                    run[base + j + h] = carry
+            return carry
 
         return lax.fori_loop(start, stop, some, carry)
 
     steps = tiles // UNROLL
-    middle = steps // SPLIT
-    carry = (jnp.zeros((2 * comps, TILE), f32), jnp.int32(-1))
+    middle = steps * SPLIT[0] // SPLIT[1]
+    carry = jnp.zeros((2 * comps, TILE), f32)
     carry = run_tiles(run1, lambda s: both16[s], 0, middle, carry)
     relay(0)
     send_loose(1)
@@ -310,8 +302,8 @@
         return change, total
 
     old0 = lambda b: fac[:, b * TILE:(b + 1) * TILE]
-    partial([(k, extra(k, take_firm(0, k))) for k in firm], lambda b: run1[loc[0, b], :comps])
-    found = [(k, extra(k, take_loose(0, n))) for n, k in enumerate(loose)]
+    partial([(k, extra(k, got)) for k, got in take_firm(0).items()], lambda b: run1[loc[0, b], :comps])
+    found = [(k, extra(k, got)) for k, got in take_loose(0).items()]
 
     def keep_upd(b, updated):
         upd3[b] = updated
@@ -321,29 +313,28 @@
             pack[2, g // 2 + i // 4] = doubled(jnp.concatenate(news[i:i + 4], axis=1))
 
     change, total = finish(found, lambda b: blend3[b], old0, keep_upd, pack_upd)
-    stat_send(0, change, total)
-
     for k in loose:
         gather(2, k)
     send_loose(2)
+    stat_send(0, change, total)
     for k in firm:
         gather(2, k)
     send_firm(2)
-    carry = (jnp.zeros((comps, TILE), f32), jnp.int32(-1))
-    run_tiles(run2, lambda s: upd3[s], 0, steps, carry)
     relay(1)
+    run_tiles(run2, lambda s: upd3[s], 0, steps, jnp.zeros((comps, TILE), f32))
     relay(2)
     beta, _ = stat_take(0)
 
     def mix(new, old):
         return (1.0 + beta) * new - beta * old
 
-    def mixed(get, k):
-        return mix(get(2, k).astype(f32), get(1, k).astype(f32)).astype(bf16)
-
-    partial([(k, extra(k, mixed(take_firm, k))) for k in firm],
+    def mixed(get):
+        old = get(1)
+        return {k: mix(new.astype(f32), old[k].astype(f32)).astype(bf16) for k, new in get(2).items()}
+
+    partial([(k, extra(k, got)) for k, got in mixed(take_firm).items()],
             lambda b: mix(run2[loc[0, b]], run1[loc[0, b], comps:]))
-    found = [(k, extra(k, mixed(take_loose, n))) for n, k in enumerate(loose)]
+    found = [(k, extra(k, got)) for k, got in mixed(take_loose).items()]
     outs = []
 
     def keep_out(b, updated):
@@ -362,7 +353,7 @@
     energy_ref[...] = jnp.broadcast_to(energy, energy_ref.shape)
     for copy in outs:
         copy.wait()
-    for copy in started:
+    for copy in pending:
         copy.wait_send()
 
 
@@ -378,24 +369,24 @@
     vm, sm, dma = pltpu.VMEM, pltpu.SMEM, pltpu.SemaphoreType.DMA
     table = -(-blocks // TILE) * TILE
     args = (factor, prior, tile_src, tile_dst, tile_count, tile_vals, sep_idx, sep_count, couple, masks)
+    args = [a if a.size == 1 else pltpu.with_memory_space_constraint(a[None] if a.ndim == 1 else a, pltpu.HBM) for a in args]
     result, beta, energy = pl.pallas_call(
         functools.partial(kernel, rows, cols, nodes * parts),
         out_shape=[jax.ShapeDtypeStruct((comps, nodes), f32)] + [jax.ShapeDtypeStruct((1, TILE), f32)] * 2,
-        in_specs=[pl.BlockSpec(memory_space=pl.ANY)] * len(args),
+        in_specs=[pl.BlockSpec(memory_space=pltpu.HBM)] * len(args),
         out_specs=[pl.BlockSpec(memory_space=pl.ANY)] + [pl.BlockSpec(memory_space=pltpu.VMEM)] * 2,
         scratch_shapes=[
             vm((comps, nodes), f32), vm((comps, nodes), f32), vm((1, tiles), i32), vm((1, tiles), i32), sm((1,), i32),
-            vm(tile_vals.shape, bf16), vm((rounds, slots), i32), sm((1, rounds), i32), vm((rounds, slots, slots), bf16), sm((rounds,), i32),
-            vm((1, tiles), i32), vm((1, table), i32), sm((1, tiles), i32), sm((1, table), i32), vm((rounds, WIDE, slots), bf16),
+            vm(tile_vals.shape, bf16), vm((rounds, slots), i32), sm((1, rounds), i32), vm((rounds, slots, slots), bf16), sm((1, rounds), i32),
+            vm((3, tiles), i32), vm((1, table), i32), sm((3, tiles), i32), sm((1, table), i32), vm((rounds, WIDE, slots), bf16),
             vm((blocks, comps, TILE), f32), vm((blocks, comps, TILE), f32), vm((blocks, comps, TILE), f32),
             vm((blocks, 2 * comps, TILE), bf16), vm((3, supers // 2, 2 * comps, WIDE), bf16),
             vm((tiles + 1, 2 * comps, TILE), f32), vm((tiles + 1, comps, TILE), f32),
-            vm((3, rounds, comps, slots), bf16), vm((3, rounds, comps, slots), bf16),
+            vm((3, rounds, comps, slots), bf16), vm((3, rounds - loose, comps, slots), bf16),
             vm((3, loose, comps, slots), bf16), vm((2, parts, 1, TILE), f32),
             *[vm((loose, cols, comps, slots), bf16)] * 3, *[vm((loose, rows, comps, slots), bf16)] * 3,
-            dma((9,)), dma((PIECES,)), dma((2,)), dma((supers // GROUP,)),
-            dma((3, rounds)), dma((3, rounds)), dma((3, loose, cols)), dma((3, loose, cols)), dma((3, loose, rows)), dma((3, loose, rows)),
-            dma((2, parts)), dma((2, parts)),
+            dma((len(args),)), dma((2,)), dma((supers // GROUP,)),
+            dma((3,)), dma((3,)), dma((3, loose)), dma((3, loose)), dma((3, loose)), dma((3, loose)), dma((2,)), dma((2,)),
         ],
         compiler_params=pltpu.CompilerParams(collective_id=0, has_side_effects=True, vmem_limit_bytes=LIMIT),
         name="rounds",

time: 44.6 us -> 35.1 us (0.79)
  Pallas kernels: 37.6 us -> 30.4 us
  local copies, waits for them, and re-layouts: 2.06 us -> 0.88 us
  between operations: 4.73 us -> 3.61 us
    pallas_call x1, Pallas kernels: 37.6 us -> 30.4 us  [local(): pl.pallas_call(functools.partial(kernel, rows, cols, nodes * parts), out_...]
    unnamed x1, local copies, waits for them, and re-layouts: 2.06 us -> 0.88 us
where the time goes in v2:
time: 35.1 us; the launch traced here: 34.9 us
  Pallas kernels  30.4 us (87%)
  between operations  3.61 us (10%)
  local copies, waits for them, and re-layouts  0.88 us (3%)
    pallas_call x1, Pallas kernels, local(): pl.pallas_call(functools.partial(kernel, rows, cols, nodes * parts), out_...  30.4 us
    unnamed x1, local copies, waits for them, and re-layouts  0.88 us

profile of v2, /device:TPU:0, one launch (start us, length us, event | category | flops | bytes accessed | tf_op | source)
XLA Modules:
  0.0 34.9 jit_solution(10226525426357174637)
XLA Ops:
  1.3 30.4 %rounds.1 = (f32[24,8192]{1,0:T(8,128)S(1)}, f32[1,128]{1,0:T(1,128)S(1)}, f32[1,128]{1,0:T(1,128)S(1)}) custom-call(f32[24,8192]{1,0:T(8,128)} %refs_0_.1, f32[24,8192]{1,0:T(8,128)} %refs_1_.1, s32[1,384]{1,0:T(1,128)} %refs_2_.1, s32[1,384]{1,0:T(1,128)} %refs_3_.1, s32[1]{0:T(128)S(6)} %copy.16.refs_4_, bf16[384,128,128]{2,1,0:T(8,128)(2,1)} %refs_5_.1, ...), custom_call_target="tpu_custom_call" | custom-call | tf_op jit(solution)/shard_map/rounds/pallas_call | solution.py:373
  31.7 0.9 %copy.17 = f32[24,8192]{1,0:T(8,128)} copy(f32[24,8192]{1,0:T(8,128)S(1)} %get-tuple-element.12) | data formatting | bytes 1572864

commit v3 on v2

--- a/solution.py
+++ b/solution.py
@@ -12,8 +12,7 @@
 MOMENTUM_CAP = 0.9
 MESH = pl.DeviceIdType.MESH
 LIMIT = 48 * 1024 * 1024
-UNROLL = 32
-SPLIT = (3, 4)
+UNROLL = 128
 GROUP = 8
 
 
@@ -30,18 +29,18 @@
     return 1 << (n - 1).bit_length()
 
 
-def kernel(rows, cols, nodes_all, *refs):
+def kernel(rows, cols, nodes_all, turn, *refs):
     refs = list(refs)
     take = lambda n: [refs.pop(0) for _ in range(n)]
     fac_h, pri_h, src_h, dst_h, live_h, vals_h, idx_h, cnt_h, cpl_h, masks_h = take(10)
-    out_h, beta_ref, energy_ref = take(3)
+    out_ref, beta_ref, energy_ref = take(3)
     fac, pri, src, dst, live, vals, idx, cnt, cpl, masks = take(10)
-    order_v, loc_v, order, loc, lt = take(5)
+    order_v, tid, sid, keep, loc, lt = take(6)
     blend3, upd3, app3, both16, pack, run1, run2 = take(7)
-    sbuf, direct, picked, stat = take(4)
-    bcol, brow = take(3), take(3)
-    in_sem, table_sem, out_sem = take(3)
-    d_send, d_recv, c_send, c_recv, r_send, r_recv, st_send, st_recv = take(8)
+    sbuf, direct, stat = take(3)
+    around = take(3)
+    in_sem, table_sem = take(2)
+    d_send, d_recv, l_send, l_recv, st_send, st_recv, ready = take(7)
 
     parts = rows * cols
     comps, nodes = fac.shape
@@ -55,7 +54,10 @@
 
     barrier = pltpu.get_barrier_semaphore()
     everyone = [(jr, jc) for jr in range(rows) for jc in range(cols) if jr or jc]
-    for jr, jc in everyone:
+    direct_to = {(rows - 1, cols - 1), (rows // 2, 0), (0, 1)}
+    ring = {(turn, j) for j in range(cols)} - {(0, 0)}
+    greeted = sorted(direct_to | ring | {(0, j) for j in range(1, cols)} | {(j, 0) for j in range(1, rows)}, reverse=True)
+    for jr, jc in greeted:
         pl.semaphore_signal(barrier, inc=1, device_id=(flip(r, jr), flip(c, jc)), device_id_type=MESH)
 
     pairs = [(idx_h.at[0], idx), (fac_h, fac), (pri_h, pri), (cnt_h, cnt), (src_h, src), (dst_h, dst), (live_h, live),
@@ -94,7 +96,6 @@
         for i in range(4):
             part = slice(i * TILE, (i + 1) * TILE)
             blend3[4 * q + i] = b[:, part]
-            both16[4 * q + i] = jnp.concatenate([b[:, part], f[:, part]], axis=0).astype(bf16)
         return carry
 
     lax.fori_loop(0, supers // 2, begin, 0, unroll=2)
@@ -120,7 +121,8 @@
             got = jnp.dot(rows_in, one, preferred_element_type=f32)
             for i in range(GROUP):
                 total = jnp.where(where == 2 * q + i, got[i * comps:(i + 1) * comps], total)
-        sbuf[kind, k] = jnp.where(slot_range < cnt[0, k], total, 0.0).astype(bf16)
+        total = jnp.where(slot_range < cnt[0, k], total, 0.0)
+        sbuf[kind, k] = jnp.concatenate([total[:, i:i + TILE] for i in range(0, slots, TILE)], axis=0).astype(bf16)
 
     pending = []
 
@@ -140,32 +142,24 @@
             remote(sbuf.at[kind, k], direct.at[kind, m], d_send.at[kind], d_recv.at[kind], place).start()
         pending.append(firm_whole(kind))
 
-    def col_whole(kind, n):
-        return whole(bcol[kind].at[n, pl.ds(1, cols - 1)], c_send.at[kind, n], c_recv.at[kind, n])
-
-    def row_whole(kind, n):
-        return whole(brow[kind].at[n, pl.ds(1, rows - 1)], r_send.at[kind, n], r_recv.at[kind, n])
+    def loose_whole(kind, n):
+        first = 0 if turn else 1
+        return whole(around[kind].at[n, pl.ds(first, cols - first)], l_send.at[kind, n], l_recv.at[kind, n])
 
     def send_loose(kind):
         for n, k in enumerate(loose):
-            for j in range(cols - 1, 0, -1):
-                remote(sbuf.at[kind, k], bcol[kind].at[n, j], c_send.at[kind, n], c_recv.at[kind, n], (r, flip(c, j))).start()
-            pending.append(col_whole(kind, n))
-            bcol[kind][n, 0] = sbuf[kind, k]
-
-    def relay(kind):
-        for n, k in enumerate(loose):
-            col_whole(kind, n).wait_recv()
-            picked[kind, n] = bcol[kind][n, masks[0, k] % cols]
-            for j in range(rows - 1, 0, -1):
-                remote(picked.at[kind, n], brow[kind].at[n, j], r_send.at[kind, n], r_recv.at[kind, n], (flip(r, j), c)).start()
-            pending.append(row_whole(kind, n))
-            brow[kind][n, 0] = picked[kind, n]
+            for j in range(cols - 1, -1, -1):
+                if turn or j:
+                    place = (flip(r, turn), flip(c, j))
+                    remote(sbuf.at[kind, k], around[kind].at[n, j], l_send.at[kind, n], l_recv.at[kind, n], place).start()
+                else:
+                    around[kind][n, 0] = sbuf[kind, k]
+            pending.append(loose_whole(kind, n))
 
     def take_loose(kind):
         for n in range(len(loose)):
-            row_whole(kind, n).wait_recv()
-        return {k: brow[kind][n, masks[0, k] // cols] for n, k in enumerate(loose)}
+            loose_whole(kind, n).wait_recv()
+        return {k: around[kind][n, masks[0, k] % cols] for n, k in enumerate(loose)}
 
     def take_firm(kind):
         firm_whole(kind).wait_recv()
@@ -198,7 +192,9 @@
     for k in loose:
         gather(0, k)
     loads[7].wait()
-    pl.semaphore_wait(barrier, len(everyone))
+    pl.semaphore_wait(barrier, len(greeted))
+    for j in range(1, rows):
+        pl.semaphore_signal(ready, inc=1, device_id=(flip(r, j), c), device_id_type=MESH)
     send_loose(0)
     for k in firm:
         gather(0, k)
@@ -209,7 +205,7 @@
     key = jnp.where(tile_row < live[0], dst[...], blocks)
     ones = lambda mask: jnp.where(mask, 1.0, 0.0)
     across = lambda a, b: lax.dot_general(a.astype(bf16), b.astype(bf16), (((1,), (1,)), ((), ())), preferred_element_type=f32)
-    block_at = lax.broadcasted_iota(jnp.int32, (loc_v.shape[1], tiles), 0)
+    block_at = lax.broadcasted_iota(jnp.int32, (max(TILE, blocks), tiles), 0)
     same = ones(block_at == key)
     upto = ones(key <= block_at)
     left = lax.broadcasted_iota(jnp.int32, (tiles, tiles), 0)
@@ -219,19 +215,20 @@
     columns = jnp.concatenate([tile_row // TILE, tile_row % TILE, src[...], key] + [tile_row] * 4, axis=0)
     sort = across(columns.astype(f32), ones(left == rank)).astype(jnp.int32)
     within = lambda x, n: jnp.minimum(jnp.maximum(x, 0), n)
-    order_v[0:1, :] = within(sort[0:1] * TILE + sort[1:2], tiles - 1)
-    order_v[1:2, :] = within(sort[2:3], blocks - 1)
-    order_v[2:3, :] = jnp.where(sort[3:4] == pltpu.roll(sort, 1, 1)[3:4], 1, 0)
+    order_v[0] = within(sort[0:1] * TILE + sort[1:2], tiles - 1)
+    order_v[1] = within(sort[2:3], blocks - 1)
+    order_v[2] = jnp.where(sort[3:4] == pltpu.roll(sort, 1, 1)[3:4], 1, 0)
     unit = jnp.ones((8, tiles), f32)
     found_at = jnp.where(across(unit, same)[:1] > 0.0, across(unit, upto)[:1].astype(jnp.int32) - 1, tiles)
-    loc_v[...] = within(found_at, tiles)
-    tables = [pltpu.make_async_copy(order_v, order, table_sem.at[0]), pltpu.make_async_copy(loc_v, loc, table_sem.at[1])]
+    wide = jnp.concatenate([within(found_at, tiles)] * (-(-tiles // found_at.shape[1])), axis=1)
+    order_v[3] = wide[:, :tiles]
+    tables = [pltpu.make_async_copy(order_v.at[i, 0], t, table_sem.at[i]) for i, t in enumerate((tid, sid, keep, loc))]
     for copy in tables:
         copy.start()
     for k in loose + firm:
         gather(1, k)
-    run1[tiles] = jnp.zeros((2 * comps, TILE), f32)
-    run2[tiles] = jnp.zeros((comps, TILE), f32)
+    run1[tiles] = jnp.zeros((comps, TILE), f32)
+    run2[tiles] = jnp.zeros((2 * comps, TILE), f32)
     for copy in tables + loads[9:]:
         copy.wait()
 
@@ -239,29 +236,27 @@
         def some(i, carry):
             base = i * UNROLL
             for j in range(0, UNROLL, 2):
-                x = jnp.concatenate([source(order[1, base + j + h]) for h in range(2)], axis=0).astype(bf16)
-                side = jnp.concatenate([vals[order[0, base + j + h]] for h in range(2)], axis=1)
+                x = jnp.concatenate([source(sid[base + j + h]) for h in range(2)], axis=0).astype(bf16)
+                side = jnp.concatenate([vals[tid[base + j + h]] for h in range(2)], axis=1)
                 got = jnp.dot(x, side, preferred_element_type=f32)
                 n = x.shape[0] // 2
                 for h in range(2):
-                    carry = jnp.where(order[2, base + j + h] > 0, carry, 0.0) + got[h * n:(h + 1) * n, h * TILE:(h + 1) * TILE]
+                    carry = jnp.where(keep[base + j + h] > 0, carry, 0.0) + got[h * n:(h + 1) * n, h * TILE:(h + 1) * TILE]
                     run[base + j + h] = carry
             return carry
 
         return lax.fori_loop(start, stop, some, carry)
 
-    steps = tiles // UNROLL
-    middle = steps * SPLIT[0] // SPLIT[1]
-    carry = jnp.zeros((2 * comps, TILE), f32)
-    carry = run_tiles(run1, lambda s: both16[s], 0, middle, carry)
-    relay(0)
     send_loose(1)
     send_firm(1)
-    run_tiles(run1, lambda s: both16[s], middle, steps, carry)
+    steps = tiles // UNROLL
+    run_tiles(run1, lambda s: blend3[s], 0, steps, jnp.zeros((comps, TILE), f32))
     loads[8].wait()
 
     def extra(k, received):
-        e = jnp.dot(received, cpl[k], preferred_element_type=f32)
+        e = 0.0
+        for i in range(slots // TILE):
+            e = e + jnp.dot(received, cpl[k, i * TILE:(i + 1) * TILE], preferred_element_type=f32)[i * comps:(i + 1) * comps]
         return jnp.where(slot_range < cnt[0, k], e, 0.0)
 
     def scatter(first, found):
@@ -302,27 +297,27 @@
         return change, total
 
     old0 = lambda b: fac[:, b * TILE:(b + 1) * TILE]
-    partial([(k, extra(k, got)) for k, got in take_firm(0).items()], lambda b: run1[loc[0, b], :comps])
+    partial([(k, extra(k, got)) for k, got in take_firm(0).items()], lambda b: run1[loc[b]])
     found = [(k, extra(k, got)) for k, got in take_loose(0).items()]
 
     def keep_upd(b, updated):
         upd3[b] = updated
+        both16[b] = jnp.concatenate([updated, old0(b)], axis=0).astype(bf16)
 
     def pack_upd(g, news):
         for i in range(0, len(news), 4):
             pack[2, g // 2 + i // 4] = doubled(jnp.concatenate(news[i:i + 4], axis=1))
 
     change, total = finish(found, lambda b: blend3[b], old0, keep_upd, pack_upd)
+    pl.semaphore_wait(ready, rows - 1)
+    stat_send(0, change, total)
     for k in loose:
         gather(2, k)
     send_loose(2)
-    stat_send(0, change, total)
     for k in firm:
         gather(2, k)
     send_firm(2)
-    relay(1)
-    run_tiles(run2, lambda s: upd3[s], 0, steps, jnp.zeros((comps, TILE), f32))
-    relay(2)
+    run_tiles(run2, lambda s: both16[s], 0, steps, jnp.zeros((2 * comps, TILE), f32))
     beta, _ = stat_take(0)
 
     def mix(new, old):
@@ -333,26 +328,17 @@
         return {k: mix(new.astype(f32), old[k].astype(f32)).astype(bf16) for k, new in get(2).items()}
 
     partial([(k, extra(k, got)) for k, got in mixed(take_firm).items()],
-            lambda b: mix(run2[loc[0, b]], run1[loc[0, b], comps:]))
+            lambda b: mix(run2[loc[b], :comps], run2[loc[b], comps:]))
     found = [(k, extra(k, got)) for k, got in mixed(take_loose).items()]
-    outs = []
 
     def keep_out(b, updated):
-        pri[:, b * TILE:(b + 1) * TILE] = updated
-
-    def write_out(g, news):
-        span = pl.ds(g * WIDE, GROUP * WIDE)
-        copy = pltpu.make_async_copy(pri.at[:, span], out_h.at[:, span], out_sem.at[g // GROUP])
-        copy.start()
-        outs.append(copy)
-
-    change, total = finish(found, lambda b: upd3[b] + beta * (upd3[b] - old0(b)), lambda b: upd3[b], keep_out, write_out)
+        out_ref[:, b * TILE:(b + 1) * TILE] = updated
+
+    change, total = finish(found, lambda b: upd3[b] + beta * (upd3[b] - old0(b)), lambda b: upd3[b], keep_out, lambda g, news: None)
     stat_send(1, change, total)
     beta, energy = stat_take(1)
     beta_ref[...] = jnp.broadcast_to(beta, beta_ref.shape)
     energy_ref[...] = jnp.broadcast_to(energy, energy_ref.shape)
-    for copy in outs:
-        copy.wait()
     for copy in pending:
         copy.wait_send()
 
@@ -365,32 +351,33 @@
     _, rounds, slots = sep_idx.shape
     parts = rows * cols
     loose = max(rounds - 3, 1)
+    flat = (comps * slots // TILE, TILE)
     f32, bf16, i32 = jnp.float32, jnp.bfloat16, jnp.int32
     vm, sm, dma = pltpu.VMEM, pltpu.SMEM, pltpu.SemaphoreType.DMA
-    table = -(-blocks // TILE) * TILE
     args = (factor, prior, tile_src, tile_dst, tile_count, tile_vals, sep_idx, sep_count, couple, masks)
     args = [a if a.size == 1 else pltpu.with_memory_space_constraint(a[None] if a.ndim == 1 else a, pltpu.HBM) for a in args]
-    result, beta, energy = pl.pallas_call(
-        functools.partial(kernel, rows, cols, nodes * parts),
+    run = lambda turn: pl.pallas_call(
+        functools.partial(kernel, rows, cols, nodes * parts, turn),
         out_shape=[jax.ShapeDtypeStruct((comps, nodes), f32)] + [jax.ShapeDtypeStruct((1, TILE), f32)] * 2,
         in_specs=[pl.BlockSpec(memory_space=pltpu.HBM)] * len(args),
-        out_specs=[pl.BlockSpec(memory_space=pl.ANY)] + [pl.BlockSpec(memory_space=pltpu.VMEM)] * 2,
+        out_specs=[pl.BlockSpec(memory_space=pltpu.VMEM)] * 3,
         scratch_shapes=[
             vm((comps, nodes), f32), vm((comps, nodes), f32), vm((1, tiles), i32), vm((1, tiles), i32), sm((1,), i32),
             vm(tile_vals.shape, bf16), vm((rounds, slots), i32), sm((1, rounds), i32), vm((rounds, slots, slots), bf16), sm((1, rounds), i32),
-            vm((3, tiles), i32), vm((1, table), i32), sm((3, tiles), i32), sm((1, table), i32), vm((rounds, WIDE, slots), bf16),
+            vm((4, 1, tiles), i32), *[sm((tiles,), i32)] * 4, vm((rounds, WIDE, slots), bf16),
             vm((blocks, comps, TILE), f32), vm((blocks, comps, TILE), f32), vm((blocks, comps, TILE), f32),
             vm((blocks, 2 * comps, TILE), bf16), vm((3, supers // 2, 2 * comps, WIDE), bf16),
-            vm((tiles + 1, 2 * comps, TILE), f32), vm((tiles + 1, comps, TILE), f32),
-            vm((3, rounds, comps, slots), bf16), vm((3, rounds - loose, comps, slots), bf16),
-            vm((3, loose, comps, slots), bf16), vm((2, parts, 1, TILE), f32),
-            *[vm((loose, cols, comps, slots), bf16)] * 3, *[vm((loose, rows, comps, slots), bf16)] * 3,
-            dma((len(args),)), dma((2,)), dma((supers // GROUP,)),
-            dma((3,)), dma((3,)), dma((3, loose)), dma((3, loose)), dma((3, loose)), dma((3, loose)), dma((2,)), dma((2,)),
+            vm((tiles + 1, comps, TILE), f32), vm((tiles + 1, 2 * comps, TILE), f32),
+            vm((3, rounds, *flat), bf16), vm((3, rounds - loose, *flat), bf16),
+            vm((2, parts, 1, TILE), f32),
+            *[vm((loose, cols, *flat), bf16)] * 3,
+            dma((len(args),)), dma((4,)),
+            dma((3,)), dma((3,)), dma((3, loose)), dma((3, loose)), dma((2,)), dma((2,)), pltpu.SemaphoreType.REGULAR,
         ],
-        compiler_params=pltpu.CompilerParams(collective_id=0, has_side_effects=True, vmem_limit_bytes=LIMIT),
+        compiler_params=pltpu.CompilerParams(collective_id=turn, has_side_effects=True, vmem_limit_bytes=LIMIT),
         name="rounds",
-    )(*args)
+    )
+    result, beta, energy = lax.switch(lax.shift_right_logical(masks[2], cols.bit_length() - 1), [run(turn) for turn in range(rows)], *args)
     return result, beta[0, 0], energy[0, 0]
 
 

time: 35.1 us -> 32.9 us (0.937); the launches traced: 34.9 us -> 33.1 us
  Pallas kernels: 30.4 us -> 26.5 us
  local copies, waits for them, and re-layouts: 0.88 us -> 2.12 us
  loops' own time: 0 us -> 0.81 us
    pallas_call x1, Pallas kernels: 30.4 us -> 26.5 us  [local(): lax.switch(lax.shift_right_logical(masks[2], cols.bit_length() - 1), [run...]
    slice x0 -> x1, local copies, waits for them, and re-layouts: none -> 1.24 us  [local(): masks[2]]
    another operation x0 -> x1, loops' own time: none -> 0.81 us  [local(): lax.switch(lax.shift_right_logical(masks[2], cols.bit_length() - 1), [run...]
where the time goes in v3:
time: 32.9 us; the launch traced here: 33.1 us
  Pallas kernels  26.5 us (81%)
  between operations  3.62 us (11%)
  local copies, waits for them, and re-layouts  2.12 us (6%)
  loops' own time  0.81 us (2%)
    pallas_call x1, Pallas kernels, local(): lax.switch(lax.shift_right_logical(masks[2], cols.bit_length() - 1), [run...  26.5 us
    slice x1, local copies, waits for them, and re-layouts, local(): masks[2]  1.24 us
    unnamed x1, local copies, waits for them, and re-layouts  0.88 us
    another operation x1, loops' own time, local(): lax.switch(lax.shift_right_logical(masks[2], cols.bit_length() - 1), [run...  0.81 us

profile of v3, /device:TPU:0, one launch (start us, length us, event | category | flops | bytes accessed | tf_op | source)
XLA Modules:
  0.0 33.1 jit_solution(11065935121774652621)
XLA Ops:
  0.6 1.2 %slice.29 = s32[1]{0:T(128)} slice(s32[4]{0:T(128)} %param.23), slice={[2:3]} | slice | bytes 8 | tf_op jit(solution)/shard_map/slice | solution.py:380
  2.5 27.4 %conditional.1 = ((f32[24,8192]{1,0:T(8,128)S(1)}, f32[1,128]{1,0:T(1,128)S(1)}, f32[1,128]{1,0:T(1,128)S(1)})) conditional(s32[]{:T(128)} %bitcast, (f32[24,8192]{1,0:T(8,128)}, f32[24,8192]{1,0:T(8,128)}, s32[1,384]{1,0:T(1,128)}, s32[1,384]{1,0:T(1,128)}, s32[1]{0:T(128)}, ...), branch_computations={%region_0.0_spmd, %region_1.0_spmd, %region_2.0_spmd, %region_3.0_... | conditional | bytes 8 | solution.py:380
  3.0 26.5 %rounds.7 = (f32[24,8192]{1,0:T(8,128)S(1)}, f32[1,128]{1,0:T(1,128)S(1)}, f32[1,128]{1,0:T(1,128)S(1)}) custom-call(f32[24,8192]{1,0:T(8,128)} %get-tuple-element.133.refs_0_, f32[24,8192]{1,0:T(8,128)} %get-tuple-element.134.refs_1_, s32[1,384]{1,0:T(1,128)} %get-tuple-element.135.refs_2_, s32[1,384]{1,0:T(1,128)} %get-tuple-element.136.refs_3_, ...), custom_call_target="tpu_custom_call" | custom-call | tf_op jit(solution)/shard_map/cond/branch_3_fun/rounds/pallas_call | solution.py:380
  29.9 0.9 %copy.28 = f32[24,8192]{1,0:T(8,128)} copy(f32[24,8192]{1,0:T(8,128)S(1)} %get-tuple-element.172) | data formatting | bytes 1572864

commit v4 on v3

--- a/solution.py
+++ b/solution.py
@@ -136,11 +136,12 @@
     def firm_whole(kind):
         return whole(direct.at[kind], d_send.at[kind], d_recv.at[kind])
 
-    def send_firm(kind):
-        for m, k in enumerate(firm):
+    def send_firm(kind, some):
+        for k in some:
             place = (flip(r, fixed(k) // cols), flip(c, fixed(k) % cols))
-            remote(sbuf.at[kind, k], direct.at[kind, m], d_send.at[kind], d_recv.at[kind], place).start()
-        pending.append(firm_whole(kind))
+            remote(sbuf.at[kind, k], direct.at[kind, firm.index(k)], d_send.at[kind], d_recv.at[kind], place).start()
+
+    far, near = firm[:1], firm[1:]
 
     def loose_whole(kind, n):
         first = 0 if turn else 1
@@ -189,16 +190,18 @@
         energy = jnp.sum(jnp.where(half, 0.0, sums), axis=1, keepdims=True)
         return MOMENTUM_CAP * 0.5 * (1.0 + jnp.tanh(change)), energy
 
-    for k in loose:
+    for k in far + loose:
         gather(0, k)
     loads[7].wait()
     pl.semaphore_wait(barrier, len(greeted))
     for j in range(1, rows):
         pl.semaphore_signal(ready, inc=1, device_id=(flip(r, j), c), device_id_type=MESH)
+    send_firm(0, far)
     send_loose(0)
-    for k in firm:
+    for k in near:
         gather(0, k)
-    send_firm(0)
+    send_firm(0, near)
+    pending.append(firm_whole(0))
     for copy in loads[4:7]:
         copy.wait()
     tile_row = lax.broadcasted_iota(jnp.int32, (1, tiles), 1)
@@ -247,10 +250,13 @@
 
         return lax.fori_loop(start, stop, some, carry)
 
+    steps = tiles // UNROLL
+    middle = steps * 2 // 3
+    carry = run_tiles(run1, lambda s: blend3[s], 0, middle, jnp.zeros((comps, TILE), f32))
     send_loose(1)
-    send_firm(1)
-    steps = tiles // UNROLL
-    run_tiles(run1, lambda s: blend3[s], 0, steps, jnp.zeros((comps, TILE), f32))
+    send_firm(1, firm)
+    pending.append(firm_whole(1))
+    run_tiles(run1, lambda s: blend3[s], middle, steps, carry)
     loads[8].wait()
 
     def extra(k, received):
@@ -311,12 +317,16 @@
     change, total = finish(found, lambda b: blend3[b], old0, keep_upd, pack_upd)
     pl.semaphore_wait(ready, rows - 1)
     stat_send(0, change, total)
+    for k in far:
+        gather(2, k)
+    send_firm(2, far)
     for k in loose:
         gather(2, k)
     send_loose(2)
-    for k in firm:
+    for k in near:
         gather(2, k)
-    send_firm(2)
+    send_firm(2, near)
+    pending.append(firm_whole(2))
     run_tiles(run2, lambda s: both16[s], 0, steps, jnp.zeros((2 * comps, TILE), f32))
     beta, _ = stat_take(0)
 

time: 32.9 us -> 31.7 us (0.964); the launches traced: 33.1 us -> 31.5 us
  Pallas kernels: 26.5 us -> 25 us
    pallas_call x1, Pallas kernels: 26.5 us -> 25 us  [local(): lax.switch(lax.shift_right_logical(masks[2], cols.bit_length() - 1), [run...]
where the time goes in v4:
time: 31.7 us; the launch traced here: 31.5 us
  Pallas kernels  25 us (79%)
  between operations  3.62 us (11%)
  local copies, waits for them, and re-layouts  2.12 us (7%)
  loops' own time  0.73 us (2%)
    pallas_call x1, Pallas kernels, local(): lax.switch(lax.shift_right_logical(masks[2], cols.bit_length() - 1), [run...  25 us
    slice x1, local copies, waits for them, and re-layouts, local(): masks[2]  1.24 us
    unnamed x1, local copies, waits for them, and re-layouts  0.88 us
    another operation x1, loops' own time, local(): lax.switch(lax.shift_right_logical(masks[2], cols.bit_length() - 1), [run...  0.73 us

profile of v4, /device:TPU:0, one launch (start us, length us, event | category | flops | bytes accessed | tf_op | source)
XLA Modules:
  0.0 31.5 jit_solution(13003674816827954208)
XLA Ops:
  0.6 1.2 %slice.29 = s32[1]{0:T(128)} slice(s32[4]{0:T(128)} %param.23), slice={[2:3]} | slice | bytes 8 | tf_op jit(solution)/shard_map/slice | solution.py:390
  2.5 25.7 %conditional.1 = ((f32[24,8192]{1,0:T(8,128)S(1)}, f32[1,128]{1,0:T(1,128)S(1)}, f32[1,128]{1,0:T(1,128)S(1)})) conditional(s32[]{:T(128)} %bitcast, (f32[24,8192]{1,0:T(8,128)}, f32[24,8192]{1,0:T(8,128)}, s32[1,384]{1,0:T(1,128)}, s32[1,384]{1,0:T(1,128)}, s32[1]{0:T(128)}, ...), branch_computations={%region_0.0_spmd, %region_1.0_spmd, %region_2.0_spmd, %region_3.0_... | conditional | bytes 8 | solution.py:390
  2.7 25.0 %rounds.5 = (f32[24,8192]{1,0:T(8,128)S(1)}, f32[1,128]{1,0:T(1,128)S(1)}, f32[1,128]{1,0:T(1,128)S(1)}) custom-call(f32[24,8192]{1,0:T(8,128)} %get-tuple-element.107.refs_0_, f32[24,8192]{1,0:T(8,128)} %get-tuple-element.108.refs_1_, s32[1,384]{1,0:T(1,128)} %get-tuple-element.109.refs_2_, s32[1,384]{1,0:T(1,128)} %get-tuple-element.110.refs_3_, ...), custom_call_target="tpu_custom_call" | custom-call | tf_op jit(solution)/shard_map/cond/branch_1_fun/rounds/pallas_call | solution.py:390
  28.2 0.9 %copy.28 = f32[24,8192]{1,0:T(8,128)} copy(f32[24,8192]{1,0:T(8,128)S(1)} %get-tuple-element.172) | data formatting | bytes 1572864
